TPU v7x, 32 devices: a whole 2x2x4 slice. The times are simulated.
32 devices in a mesh: cuts: 4 (over x, core), fiber: 8 (over z, y).
Axes of the slice: x: 2, y: 2, z: 4, core: 2. Of those that a mesh axis runs over, the one named last changes fastest.
Arguments:
- tile_vals: bfloat16 [131072, 128], P(('cuts', 'fiber')), may hold values from -6 to 6
- tile_count: int32 [131072], P(('cuts', 'fiber')), may hold values from 1 to 128
- tile_dest: int32 [131072, 1], P(('cuts', 'fiber')), may hold values from 0 to 3; in each aligned block of 4096 rows (0 to 4095, 4096 to 8191, ...) at most 2048 rows name the same one
- tile_row: int32 [131072], P(('cuts', 'fiber')), may hold values from 0 to 1023, as said below
- tile_block: int32 [131072], P(('cuts', 'fiber')), may hold values from 0 to 3
- tile_first: int32 [131072], P(('cuts', 'fiber')), may hold values from 0 to 255
- factor_one: bfloat16 [8192, 32], P(('cuts', 'fiber')), may hold values from -1.5 to 1.5
- factor_three: bfloat16 [4096, 32], P('fiber'), may hold values from -0.5 to 0.5
- factor_two: bfloat16 [4096, 32], P(('cuts', 'fiber')), may hold values from -0.09375 to 0.09375
Outputs:
- ttmc: bfloat16 [4096, 1024], P(('cuts', 'fiber'))
- projected: float32 [4096, 32], P(('cuts', 'fiber'))
Inputs may be any that keep to these rules, and one draw needn't show every extreme that they name: `tile_dest`: among the tiles of one device, each index of cuts is named at most 2048 times, and exactly 2048 times by some. `tile_row`: among the tiles of one device, each block of 128 consecutive values (starting at multiples of 128) is taken exactly 512 times.
All inputs are finite; a program needn't handle non-finite values.
Results may differ from a plain program's by a relative error of at most 0.002.
Values may be sent and summed in bfloat16 or wider, within the bound.
A program may use at most 128 MiB of HBM per device.

v0:
```python
import jax
import jax.numpy as jnp
from jax import lax
from jax.sharding import PartitionSpec as P

R1 = 32
R3 = 32
FIBER = 128
I2_DEV = 1024


def project_tiles(values, block_ids, factor_three):
    blocks = factor_three.shape[0] // FIBER
    table = factor_three.reshape(blocks, FIBER, R3).transpose(1, 0, 2).reshape(FIBER, blocks * R3)
    every = jnp.dot(values, table, preferred_element_type=jnp.float32).reshape(
        values.shape[0], blocks, R3
    )
    pick = (block_ids[:, None] == jnp.arange(blocks, dtype=jnp.int32)[None, :]).astype(jnp.float32)
    return jnp.sum(every * pick[:, :, None], axis=1)


def slot_of(owners, owner_count, capacity):
    member = (owners[:, None] == jnp.arange(owner_count, dtype=jnp.int32)[None, :]).astype(
        jnp.int32
    )
    before = jnp.cumsum(member, axis=0) - member
    return owners * capacity + jnp.sum(before * member, axis=1)


def place_into(values, slot_ids, owner_count, capacity):
    buffer = jnp.zeros((owner_count * capacity,) + values.shape[1:], values.dtype)
    return buffer.at[slot_ids].set(values).reshape((owner_count, capacity) + values.shape[1:])


def body(
    tile_vals,
    tile_count,
    tile_dest,
    tile_row,
    tile_block,
    tile_first,
    factor_one,
    factor_three,
    factor_two,
):
    ncuts = lax.axis_size("cuts")
    tiles = tile_vals.shape[0]
    positions = jnp.arange(FIBER, dtype=jnp.int32)
    masked = jnp.where(
        positions[None, :] < tile_count[:, None], tile_vals, jnp.zeros_like(tile_vals)
    )
    dest = tile_dest[:, 0]
    first_rows = jnp.take(factor_one, tile_first, axis=0)
    fiber_count = lax.axis_size("fiber")
    block_rows = I2_DEV // fiber_count
    fiber_cap = tiles // fiber_count
    fiber_slots = fiber_count * fiber_cap
    row_owner = tile_row // block_rows
    fiber_slot = slot_of(row_owner, fiber_count, fiber_cap)
    local_proj = project_tiles(masked, tile_block, factor_three)
    first_wide = first_rows.astype(jnp.float32)
    combined = dest * block_rows + tile_row % block_rows
    got_proj, got_first, got_rows = (
        lax.all_to_all(
            place_into(local_proj, fiber_slot, fiber_count, fiber_cap),
            "fiber",
            split_axis=0,
            concat_axis=0,
            tiled=True,
        ),
        lax.all_to_all(
            place_into(first_wide, fiber_slot, fiber_count, fiber_cap),
            "fiber",
            split_axis=0,
            concat_axis=0,
            tiled=True,
        ),
        lax.all_to_all(
            place_into(combined[:, None], fiber_slot, fiber_count, fiber_cap),
            "fiber",
            split_axis=0,
            concat_axis=0,
            tiled=True,
        ),
    )
    proj = got_proj.reshape(fiber_slots, R3)
    first_f = got_first.reshape(fiber_slots, R1)
    target = got_rows.reshape(fiber_slots)
    kron = (first_f[:, :, None] * proj[:, None, :]).reshape(fiber_slots, R1 * R3)
    partial_rows = jax.ops.segment_sum(kron, target, num_segments=ncuts * block_rows)
    summed = lax.psum_scatter(partial_rows, "cuts", scatter_dimension=0, tiled=True)
    ttmc = summed.astype(jnp.bfloat16)
    local_gram = lax.dot_general(
        ttmc, factor_two, (((0,), (0,)), ((), ())), preferred_element_type=jnp.float32
    )
    gram = lax.psum(local_gram, ("cuts", "fiber"))
    gram_b = gram.astype(jnp.bfloat16)
    projected = jnp.dot(ttmc, gram_b, preferred_element_type=jnp.float32) / 32.0
    return (ttmc, projected)


def solution(mesh):
    in_specs = (
        P(("cuts", "fiber"), None),
        P(("cuts", "fiber")),
        P(("cuts", "fiber"), None),
        P(("cuts", "fiber")),
        P(("cuts", "fiber")),
        P(("cuts", "fiber")),
        P(("cuts", "fiber"), None),
        P("fiber", None),
        P(("cuts", "fiber"), None),
    )
    out_specs = (P(("cuts", "fiber"), None), P(("cuts", "fiber"), None))
    return jax.shard_map(body, mesh=mesh, in_specs=in_specs, out_specs=out_specs, check_vma=False)
```

profile of v0, /device:TPU:0, one launch (start us, length us, event | category | flops | bytes accessed | tf_op | source)
XLA Modules:
  0.0 238.0 jit_solution(2505887969231628959)
XLA Ops:
  7.2 0.0 copy-start
  7.2 0.7 broadcast_multiply_fusion.1
  7.9 0.8 reshape.76
  8.7 0.7 fusion.21
  9.4 0.7 fusion.24
  10.2 2.3 reduce-window.6
  12.5 0.3 slice_reduce_fusion
  12.8 0.2 reduce-window.9
  13.0 0.1 add_bitcast_fusion
  13.1 0.1 fusion.18
  13.2 2.2 fusion.3
  15.5 0.0 copy-start.2
  15.5 2.0 copy.31
  17.4 0.0 copy-done.2
  17.5 11.4 %scatter_custom_fusion.2 = f32[4096,32]{1,0:T(8,128)S(1)} fusion(s32[4096]{0:T(1024)S(1)} %get-tuple-element.4, f32[4096,32]{1,0:T(8,128)} %copy.31, f32[]{:T(128)} %constant.50.clone.1), kind=kCustom, calls=%fused_computation.16 | custom fusion | bytes 524800 | tf_op jit(solution)/shard_map/scatter | solution.py:32
  28.9 0.0 copy-start.3
  28.9 1.4 copy.32
  30.3 7.3 %all-to-all-start.2 = ((f32[8,512,32]{1,2,0:T(8,128)}), f32[8,512,32]{1,2,0:T(8,128)S(1)}, u32[]{:S(2)}, u32[]{:S(2)}) async-start(f32[8,512,32]{1,2,0:T(8,128)} %copy.32), calls=%async_computation.2 | async-start | bytes 1048576 | tf_op jit(solution)/shard_map/all_to_all | solution.py:64
  37.6 0.0 copy-done.3
  37.6 0.1 copy.27
  37.7 25.8 %scatter_custom_fusion.1 = f32[4096,32]{1,0:T(8,128)S(1)} fusion(s32[4096]{0:T(1024)S(1)} %get-tuple-element.4, f32[]{:T(128)} %constant.50.clone.1, pred[4096]{0:T(1024)(128)(4,1)S(1)} %compare_and_fusion, bf16[]{:T(256)} %constant.61.clone.1, bf16[256,32]{1,0:T(8,128)(2,1)S(1)} %copy.27, s32[4096]{0:T(1024)S(1)} %get-tuple-element.5), kind=kCustom, calls=%fused_computation.8 | custom fusion | flops 262144 | bytes 610310 | tf_op jit(solution)/shard_map/scatter | solution.py:32
  63.5 1.4 copy.28
  64.9 0.0 all-to-all-done.2
  64.9 6.0 %all-to-all-start.1 = ((f32[8,512,32]{1,2,0:T(8,128)}), f32[8,512,32]{1,2,0:T(8,128)S(1)}, u32[]{:S(2)}, u32[]{:S(2)}) async-start(f32[8,512,32]{1,2,0:T(8,128)} %copy.28), calls=%async_computation.1 | async-start | bytes 1048576 | tf_op jit(solution)/shard_map/all_to_all | solution.py:71
  70.9 16.1 %scatter_custom_fusion = s32[4096]{0:T(1024)} fusion(s32[4096]{0:T(1024)S(1)} %get-tuple-element.4, s32[4096]{0:T(1024)S(1)} %get-tuple-element.2, s32[]{:T(128)} %constant.51.clone.1), kind=kCustom, calls=%fused_computation.51 | custom fusion | bytes 16388 | tf_op jit(solution)/shard_map/scatter | solution.py:32
  87.0 0.0 all-to-all-done.1
  87.0 6.0 %all-to-all-start = ((s32[8,512,1]{1,2,0:T(1,128)}), s32[8,512,1]{1,2,0:T(1,128)S(1)}, u32[]{:S(2)}, u32[]{:S(2)}) async-start(s32[8,512,1]{1,2,0:T(1,128)} %bitcast.3), calls=%async_computation | async-start | bytes 32768 | tf_op jit(solution)/shard_map/all_to_all | solution.py:78
  93.0 0.2 reduce-scatter.2.cloned.1.call-start
  93.3 7.8 %broadcast_multiply_fusion = f32[4096,32,32]{0,2,1:T(8,128)} fusion(f32[4096,32]{0,1:T(8,128)S(1)} %bitcast.53, f32[4096,32]{0,1:T(8,128)S(1)} %bitcast.54), kind=kLoop, calls=%fused_computation.5 | loop fusion | flops 4194304 | bytes 17825792 | tf_op jit(solution)/shard_map/mul | solution.py:89
  101.1 17.5 %copy.34 = f32[4096,1024]{1,0:T(8,128)} copy(f32[4096,1024]{0,1:T(8,128)} %bitcast.50) | data formatting | bytes 33554432 | tf_op jit(solution)/shard_map/mul | solution.py:89
  118.6 0.0 all-to-all-done
  118.6 37.7 %scatter_custom_fusion.3 = f32[512,1024]{1,0:T(8,128)} fusion(s32[4096]{0:T(1024)S(1)} %bitcast.61, f32[4096,1024]{1,0:T(8,128)} %copy.34, f32[]{:T(128)} %constant.50.clone.1), kind=kCustom, calls=%fused_computation.19 | custom fusion | flops 4194304 | bytes 2097664 | tf_op jit(solution)/shard_map/scatter-add | solution.py:90
  156.3 0.0 reduce-scatter.2.cloned.1.call-update
  156.3 32.5 %reduce-scatter.2.cloned.1.call-done = f32[128,1024]{1,0:T(8,128)} async-done(((f32[512,1024]{1,0:T(8,128)}), f32[128,1024]{1,0:T(8,128)}) %reduce-scatter.2.cloned.1.call-update) | async-done | bytes 524304 | tf_op jit(solution)/shard_map/reduce_scatter | solution.py:91
  188.9 1.1 convert_element_type.27
  189.9 0.0 copy-done
  190.0 0.0 copy-start.1
  190.0 0.2 fusion.32
  190.1 40.2 %all-reduce.1 = bf16[1024,32]{0,1:T(8,128)(2,1)S(1)} all-reduce(f32[1024,32]{0,1:T(8,128)S(1)} %fusion.32), channel_id=1, replica_groups=mesh['cuts'=4,'fiber'=8] {'cuts','fiber'}, use_global_device_ids=true, to_apply=%region_9.10 | all-reduce | flops 32768 | bytes 196608 | tf_op jit(solution)/shard_map/psum | solution.py:96
  230.4 0.8 convolution_multiply_fusion.1
  231.2 0.0 copy-done.1
  (5 shorter events, 0.1 us)
Async XLA Ops:
  7.2 182.8 %copy-start = (bf16[128,32]{0,1:T(8,128)(2,1)S(1)}, bf16[128,32]{0,1:T(8,128)(2,1)}, u32[]{:S(2)}) copy-start(bf16[128,32]{0,1:T(8,128)(2,1)} %param.17) | copy-start | bytes 24580
  15.5 2.0 copy-start.2
  28.9 8.7 %copy-start.3 = (bf16[256,32]{0,1:T(8,128)(2,1)S(1)}, bf16[256,32]{0,1:T(8,128)(2,1)}, u32[]{:S(2)}) copy-start(bf16[256,32]{0,1:T(8,128)(2,1)} %param.15) | copy-start | bytes 49156
  30.3 34.6 %all-to-all-start.2 = ((f32[8,512,32]{1,2,0:T(8,128)}), f32[8,512,32]{1,2,0:T(8,128)S(1)}, u32[]{:S(2)}, u32[]{:S(2)}) async-start(f32[8,512,32]{1,2,0:T(8,128)} %copy.32), calls=%async_computation.2 | async-start | bytes 1048576 | tf_op jit(solution)/shard_map/all_to_all | solution.py:64
  64.9 22.1 %all-to-all-start.1 = ((f32[8,512,32]{1,2,0:T(8,128)}), f32[8,512,32]{1,2,0:T(8,128)S(1)}, u32[]{:S(2)}, u32[]{:S(2)}) async-start(f32[8,512,32]{1,2,0:T(8,128)} %copy.28), calls=%async_computation.1 | async-start | bytes 1048576 | tf_op jit(solution)/shard_map/all_to_all | solution.py:71
  87.0 31.5 %all-to-all-start = ((s32[8,512,1]{1,2,0:T(1,128)}), s32[8,512,1]{1,2,0:T(1,128)S(1)}, u32[]{:S(2)}, u32[]{:S(2)}) async-start(s32[8,512,1]{1,2,0:T(1,128)} %bitcast.3), calls=%async_computation | async-start | bytes 32768 | tf_op jit(solution)/shard_map/all_to_all | solution.py:78
  93.0 95.8 %reduce-scatter.2.cloned.1.call-start = ((), (), s32[]{:S(2)}) async-start(), calls=%async_computation.4 | async-start | bytes 2621440 | tf_op jit(solution)/shard_map/reduce_scatter | solution.py:91
  190.0 41.2 %copy-start.1 = (bf16[128,1024]{1,0:T(8,128)(2,1)}, bf16[128,1024]{1,0:T(8,128)(2,1)S(1)}, u32[]{:S(2)}) copy-start(bf16[128,1024]{1,0:T(8,128)(2,1)S(1)} %convert_element_type.27) | copy-start | bytes 786436
Sparse Core Ops, SparseCore 0:
  156.4 32.3 reduce-scatter.1
where the time goes:
time: 239 us; the launch traced here: 238 us
  other arithmetic  77.3 us (32%)
  local copies, waits for them, and re-layouts  51 us (21%)
  blocking collectives  40.2 us (17%)
  waiting for transfers between devices  32.6 us (14%)
  starting transfers between devices  19.5 us (8%)
  between operations  14.2 us (6%)
  matrix products  3.18 us (1%)
    psum x1, blocking collectives, body(): gram = lax.psum(local_gram, ('cuts', 'fiber'))  40.2 us
    scatter-add x1, other arithmetic, body(): jax.ops.segment_sum(kron, target, num_segments=ncuts * block_rows)  37.7 us
    reduce_scatter x1, waiting for transfers between devices, body(): lax.psum_scatter(partial_rows, 'cuts', scatter_dimension=0, tiled=True)  32.5 us
    scatter x2, local copies, waits for them, and re-layouts, place_into(): buffer.at[slot_ids].set(values)  27.5 us
    scatter x1, other arithmetic, place_into(): buffer.at[slot_ids].set(values)  25.8 us
    mul x3, local copies, waits for them, and re-layouts, body(): first_f[:, :, None] * proj[:, None, :]  17.5 us
    mul x1, other arithmetic, body(): first_f[:, :, None] * proj[:, None, :]  7.8 us
    all_to_all x1, starting transfers between devices, body(): lax.all_to_all(place_into(local_proj, fiber_slot, fiber_count, fiber_cap)...  7.31 us
  transfers between devices with their start and end apart: 4, of which 1 were waited for; matrix products, arithmetic and copies ran while one was open for 29% of the time, Pallas kernels for 0%

commit v1 on v0

v1 whole, which is shorter than its diff:
```python
import functools

import jax
import jax.numpy as jnp
from jax import lax
from jax.experimental import pallas as pl
from jax.experimental.pallas import tpu as pltpu
from jax.sharding import PartitionSpec as P

FIBER = 128
I2_DEV = 1024
CHUNK = 512
PARTS = 4
MESH = pl.DeviceIdType.MESH
NT = (((1,), (1,)), ((), ()))


def onehot(count, row, dtype=jnp.bfloat16):
    spots = lax.broadcasted_iota(jnp.int32, (count, row.shape[1]), 0).astype(row.dtype)
    return jnp.where(spots == row, 1.0, 0.0).astype(dtype)


def project_tiles(values, block_ids, factor_three):
    r3 = factor_three.shape[1]
    blocks = factor_three.shape[0] // FIBER
    table = factor_three.reshape(blocks, FIBER, r3).transpose(1, 0, 2).reshape(FIBER, blocks * r3)
    every = lax.dot_general(
        table, values, (((0,), (1,)), ((), ())), preferred_element_type=jnp.float32
    ).reshape(blocks, r3, values.shape[0])
    pick = (block_ids[None, :] == jnp.arange(blocks, dtype=jnp.int32)[:, None]).astype(jnp.float32)
    return jnp.sum(every * pick[:, None, :], axis=0)


def kernel(
    nc,
    nf,
    proj_ref,
    dest_ref,
    row_ref,
    first_ref,
    f1_ref,
    f2_ref,
    ttmc_ref,
    out_ref,
    data,
    member,
    slots,
    masked,
    send,
    got,
    kh,
    kl,
    acc,
    sib,
    xrecv,
    gram,
    grecv,
    gown,
    gall,
    gfull,
    a2a_send,
    a2a_recv,
    sib_send,
    sib_recv,
    x_send,
    x_recv,
    g_send,
    g_recv,
    b_send,
    b_recv,
):
    tiles = proj_ref.shape[1]
    r3 = proj_ref.shape[0]
    r1 = f1_ref.shape[0]
    r2 = f2_ref.shape[0]
    feats = data.shape[0]
    cap = tiles // nf
    br = f2_ref.shape[1]
    chunks = tiles // CHUNK
    width = r1 * r3
    nx = nc // 2
    ndev = nc * nf
    pieces = gram.shape[0]
    stride = ndev // pieces
    lanes = width // 128
    part = width // PARTS
    q = lax.axis_index("cuts")
    f = lax.axis_index("fiber")
    x = q // 2
    c = q % 2
    me = q * nf + f

    barrier = pltpu.get_barrier_semaphore()

    @pl.loop(1, ndev)
    def _(k):
        other = lax.rem(me + k, ndev)
        pl.semaphore_signal(
            barrier, inc=1, device_id=(other // nf, lax.rem(other, nf)), device_id_type=MESH
        )

    groups = lax.broadcasted_iota(jnp.int32, (nf, tiles), 0)
    owner = row_ref[...] // br
    member[...] = jnp.where(groups == owner, 1.0, 0.0)
    stacked = jnp.concatenate(
        [member[:, k * CHUNK : (k + 1) * CHUNK] for k in range(chunks)], axis=0
    )
    early = lax.broadcasted_iota(jnp.int32, (CHUNK, CHUNK), 0)
    late = lax.broadcasted_iota(jnp.int32, (CHUNK, CHUNK), 1)
    before = jnp.dot(
        stacked.astype(jnp.bfloat16),
        jnp.where(early < late, 1.0, 0.0).astype(jnp.bfloat16),
        preferred_element_type=jnp.float32,
    )
    carry = jnp.zeros((nf, 1), jnp.float32)
    for k in range(chunks):
        cols = slice(k * CHUNK, (k + 1) * CHUNK)
        mem = member[:, cols]
        rank = jnp.sum(mem * (before[k * nf : (k + 1) * nf] + carry), axis=0, keepdims=True)
        carry = carry + jnp.sum(mem, axis=1, keepdims=True)
        slots[:, cols] = onehot(cap, rank)
        value = proj_ref[:, cols]
        high = value.astype(jnp.bfloat16)
        data[0:r3, cols] = high
        data[r3 : 2 * r3, cols] = (value - high.astype(jnp.float32)).astype(jnp.bfloat16)
        data[2 * r3 : 2 * r3 + r1, cols] = jnp.dot(
            f1_ref[...],
            onehot(f1_ref.shape[1], first_ref[:, cols]),
            preferred_element_type=jnp.float32,
        ).astype(jnp.bfloat16)
        kind = lax.broadcasted_iota(jnp.int32, (16, CHUNK), 0)
        rows = row_ref[:, cols]
        marks = jnp.where(kind == 0, dest_ref[:, cols], jnp.where(kind == 1, rows % br, 0))
        data[2 * r3 + r1 :, cols] = marks.astype(jnp.float32).astype(jnp.bfloat16)

    def a2a_copy(j):
        to = lax.rem(f + j, nf)
        return pltpu.make_async_remote_copy(
            src_ref=send.at[j],
            dst_ref=got.at[j],
            send_sem=a2a_send.at[j],
            recv_sem=a2a_recv.at[j],
            device_id=(q, to),
            device_id_type=MESH,
        )

    def place(first_step):
        for half in range(2):
            group = lax.rem(f + first_step + half, nf)
            masked[half * feats : (half + 1) * feats, :] = data[...] * member[
                pl.ds(group, 1), :
            ].astype(jnp.bfloat16)
        return lax.dot_general(
            masked[...], slots[...], NT, preferred_element_type=jnp.float32
        ).astype(jnp.bfloat16)

    pl.semaphore_wait(barrier, ndev - 1)

    @pl.loop(0, nf // 2)
    def _(pair):
        j = 2 * pair + 1
        placed = place(j)
        send[j] = placed[:feats]
        a2a_copy(j).start()

        @pl.when(pair < nf // 2 - 1)
        def _():
            send[j + 1] = placed[feats:]
            a2a_copy(j + 1).start()

        @pl.when(pair == nf // 2 - 1)
        def _():
            got[0] = placed[feats:]

    def target(j, xs):
        marks = got[j, 2 * r3 + r1 :, :].astype(jnp.float32)
        key = (marks[0:1] - (2 * xs).astype(jnp.float32)) * br + marks[1:2]
        return onehot(2 * br, key)

    def add(slot, rows, total, fresh):
        for half in range(2):
            new = total[:, half * br : (half + 1) * br]
            if fresh:
                acc[slot, half, rows, :] = new
            else:
                acc[slot, half, rows, :] += new

    def sib_copy(slot, k):
        rows = pl.ds(k * part, part)
        return pltpu.make_async_remote_copy(
            src_ref=acc.at[slot, 1 - c, rows],
            dst_ref=sib.at[slot, rows],
            send_sem=sib_send.at[slot, k],
            recv_sem=sib_recv.at[slot, k],
            device_id=(x * 2 + 1 - c, f),
            device_id_type=MESH,
        )

    def x_copy(slot, k):
        rows = pl.ds(k * part, part)
        return pltpu.make_async_remote_copy(
            src_ref=acc.at[slot, c, rows],
            dst_ref=xrecv.at[slot, rows],
            send_sem=x_send.at[slot, k],
            recv_sem=x_recv.at[slot, k],
            device_id=(lax.rem(x + slot, nx) * 2 + c, f),
            device_id_type=MESH,
        )

    per = part // r3
    first_slot = 1 % nx

    def arrive(j, fresh):
        sel = target(j, lax.rem(x + first_slot, nx))
        value = got[j, 0:r3, :].astype(jnp.float32) + got[j, r3 : 2 * r3, :].astype(jnp.float32)
        fr = got[j, 2 * r3 : 2 * r3 + r1, :].astype(jnp.float32)
        for k in range(PARTS):
            rows = pl.ds(k * part, part)
            prod = jnp.concatenate(
                [fr[k * per + i : k * per + i + 1] * value for i in range(per)], axis=0
            )
            high = prod.astype(jnp.bfloat16)
            low = (prod - high.astype(jnp.float32)).astype(jnp.bfloat16)
            kh[j, rows, :] = high
            kl[j, rows, :] = low
            total = lax.dot_general(
                high, sel, NT, preferred_element_type=jnp.float32
            ) + lax.dot_general(low, sel, NT, preferred_element_type=jnp.float32)
            add(first_slot, rows, total, fresh)

    arrive(0, True)

    @pl.loop(1, nf)
    def _(j):
        a2a_copy(j).wait()
        arrive(j, False)

    def exchange(slot):
        for k in range(PARTS):
            sib_copy(slot, k).start()

    def forward(slot):
        for k in range(PARTS):
            rows = pl.ds(k * part, part)
            sib_copy(slot, k).wait()
            acc[slot, c, rows, :] += sib[slot, rows, :]
            if slot:
                x_copy(slot, k).start()

    def again(slot):
        @pl.loop(0, PARTS)
        def _(k):
            rows = pl.ds(pl.multiple_of(k * part, part), part)
            for j in range(nf):
                sel = target(j, lax.rem(x + slot, nx))
                total = lax.dot_general(
                    kh[j, rows, :], sel, NT, preferred_element_type=jnp.float32
                ) + lax.dot_general(kl[j, rows, :], sel, NT, preferred_element_type=jnp.float32)
                add(slot, rows, total, j == 0)

    exchange(first_slot)
    forward(first_slot)
    for slot in list(range(2, nx)) + ([0] if nx > 1 else []):
        again(slot)
        exchange(slot)
        forward(slot)

    for k in range(PARTS):
        rows = pl.ds(k * part, part)
        for slot in range(1, nx):
            x_copy(slot, k).wait()
        total = acc[0, c, rows, :]
        for slot in range(1, nx):
            total = total + xrecv[slot, rows, :]
        ttmc_ref[:, k * part : (k + 1) * part] = total.T.astype(jnp.bfloat16)

    ttmc = ttmc_ref[...]
    local = jnp.dot(f2_ref[...], ttmc, preferred_element_type=jnp.float32)
    for p in range(pieces):
        a, b = p // lanes, p % lanes
        gram[p] = local[a * 8 : (a + 1) * 8, b * 128 : (b + 1) * 128]

    def gram_copy(p):
        to = p * stride
        return pltpu.make_async_remote_copy(
            src_ref=gram.at[p],
            dst_ref=grecv.at[me],
            send_sem=g_send,
            recv_sem=g_recv,
            device_id=(to // nf, lax.rem(to, nf)),
            device_id_type=MESH,
        )

    def back_copy(k):
        to = lax.rem(me + k, ndev)
        return pltpu.make_async_remote_copy(
            src_ref=gown,
            dst_ref=gall.at[me // stride],
            send_sem=b_send,
            recv_sem=b_recv,
            device_id=(to // nf, lax.rem(to, nf)),
            device_id_type=MESH,
        )

    def drain(ref, count, sem):
        pltpu.make_async_copy(ref.at[pl.ds(0, count)], ref.at[pl.ds(0, count)], sem).wait()

    mine = me // stride
    owns = lax.rem(me, stride) == 0

    @pl.loop(0, pieces)
    def _(k):
        p = lax.rem(mine + k, pieces)

        @pl.when(p * stride != me)
        def _():
            gram_copy(p).start()

    @pl.when(owns)
    def _():
        grecv[me] = gram[mine]
        drain(grecv, ndev - 1, g_recv)
        gown[...] = jnp.sum(grecv[...], axis=0)
        gall[mine] = gown[...]

        @pl.loop(1, ndev)
        def _(k):
            back_copy(k).start()

        drain(gall, pieces - 1, b_recv)

    @pl.when(jnp.logical_not(owns))
    def _():
        drain(gall, pieces, b_recv)

    for p in range(pieces):
        a, b = p // lanes, p % lanes
        gfull[a * 8 : (a + 1) * 8, b * 128 : (b + 1) * 128] = gall[p]
    out_ref[...] = lax.dot_general(
        ttmc, gfull[...].astype(jnp.bfloat16), NT, preferred_element_type=jnp.float32
    ) / 32.0

    @pl.when(owns)
    def _():
        drain(gram, pieces - 1, g_send)
        drain(grecv, ndev - 1, b_send)

    @pl.when(jnp.logical_not(owns))
    def _():
        drain(gram, pieces, g_send)


def body(
    tile_vals,
    tile_count,
    tile_dest,
    tile_row,
    tile_block,
    tile_first,
    factor_one,
    factor_three,
    factor_two,
):
    nc = lax.axis_size("cuts")
    nf = lax.axis_size("fiber")
    tiles = tile_vals.shape[0]
    r1, r2, r3 = factor_one.shape[1], factor_two.shape[1], factor_three.shape[1]
    br = I2_DEV // nf
    cap = tiles // nf
    width = r1 * r3
    nx = nc // 2
    feats = 2 * r3 + r1 + 16
    pieces = (r2 // 8) * (width // 128)
    positions = jnp.arange(FIBER, dtype=jnp.int32)
    masked = jnp.where(
        positions[None, :] < tile_count[:, None], tile_vals, jnp.zeros_like(tile_vals)
    )
    proj = project_tiles(masked, tile_block, factor_three)
    vmem = pl.BlockSpec(memory_space=pltpu.VMEM)
    bf16, f32 = jnp.bfloat16, jnp.float32
    dma = pltpu.SemaphoreType.DMA
    return pl.pallas_call(
        functools.partial(kernel, nc, nf),
        out_shape=(
            jax.ShapeDtypeStruct((br, width), bf16),
            jax.ShapeDtypeStruct((br, r2), f32),
        ),
        in_specs=[vmem] * 6,
        out_specs=(vmem, vmem),
        scratch_shapes=[
            pltpu.VMEM((feats, tiles), bf16),
            pltpu.VMEM((nf, tiles), f32),
            pltpu.VMEM((cap, tiles), bf16),
            pltpu.VMEM((2 * feats, tiles), bf16),
            pltpu.VMEM((nf, feats, cap), bf16),
            pltpu.VMEM((nf, feats, cap), bf16),
            pltpu.VMEM((nf, width, cap), bf16),
            pltpu.VMEM((nf, width, cap), bf16),
            pltpu.VMEM((nx, 2, width, br), f32),
            pltpu.VMEM((nx, width, br), f32),
            pltpu.VMEM((nx, width, br), f32),
            pltpu.VMEM((pieces, 8, 128), f32),
            pltpu.VMEM((nc * nf, 8, 128), f32),
            pltpu.VMEM((8, 128), f32),
            pltpu.VMEM((pieces, 8, 128), f32),
            pltpu.VMEM((r2, width), f32),
            dma((nf,)),
            dma((nf,)),
            dma((nx, PARTS)),
            dma((nx, PARTS)),
            dma((nx, PARTS)),
            dma((nx, PARTS)),
            dma,
            dma,
            dma,
            dma,
        ],
        compiler_params=pltpu.CompilerParams(
            collective_id=0, has_side_effects=True, vmem_limit_bytes=60 * 1024 * 1024
        ),
    )(
        proj,
        tile_dest.reshape(1, tiles),
        tile_row.reshape(1, tiles),
        tile_first.reshape(1, tiles),
        factor_one.T,
        factor_two.T,
    )


def solution(mesh):
    in_specs = (
        P(("cuts", "fiber"), None),
        P(("cuts", "fiber")),
        P(("cuts", "fiber"), None),
        P(("cuts", "fiber")),
        P(("cuts", "fiber")),
        P(("cuts", "fiber")),
        P(("cuts", "fiber"), None),
        P("fiber", None),
        P(("cuts", "fiber"), None),
    )
    out_specs = (P(("cuts", "fiber"), None), P(("cuts", "fiber"), None))
    return jax.shard_map(body, mesh=mesh, in_specs=in_specs, out_specs=out_specs, check_vma=False)
```

time: 239 us -> 68.5 us (0.29)
  other arithmetic: 77.3 us -> 1.72 us
  Pallas kernels: 0 us -> 59.6 us
  local copies, waits for them, and re-layouts: 51 us -> 3.97 us
  blocking collectives: 40.2 us -> 0 us
  waiting for transfers between devices: 32.6 us -> 0 us
  starting transfers between devices: 19.5 us -> 0 us
  between operations: 14.2 us -> 0.66 us
    pallas_call x0 -> x1, Pallas kernels: none -> 59.6 us  [body(): pl.pallas_call(functools.partial(kernel, nc, nf), out_shape=(jax.ShapeDty...]
    psum x1 -> x0, blocking collectives: 40.2 us -> none  [body(): gram = lax.psum(local_gram, ('cuts', 'fiber'))]
    scatter-add x1 -> x0, other arithmetic: 37.7 us -> none  [body(): jax.ops.segment_sum(kron, target, num_segments=ncuts * block_rows)]
    reduce_scatter x1 -> x0, waiting for transfers between devices: 32.5 us -> none  [body(): lax.psum_scatter(partial_rows, 'cuts', scatter_dimension=0, tiled=True)]
    scatter x2 -> x0, local copies, waits for them, and re-layouts: 27.5 us -> none  [place_into(): buffer.at[slot_ids].set(values)]
    scatter x1 -> x0, other arithmetic: 25.8 us -> none  [place_into(): buffer.at[slot_ids].set(values)]
    all_to_all x3 -> x0, starting transfers between devices: 19.3 us -> none  [the longest x1 7.31 us: body(): lax.all_to_all(place_into(local_proj, fiber_slot, fiber_count, fiber_cap)...]
    mul x3 -> x0, local copies, waits for them, and re-layouts: 17.5 us -> none  [body(): first_f[:, :, None] * proj[:, None, :]]
  transfers between devices with their start and end apart: 4 -> 0, of which waited for: 1 -> 0; matrix products, arithmetic and copies ran while one was open for 29% -> 0% of each run, Pallas kernels for 0% -> 0%
where the time goes in v1:
time: 68.5 us; the launch traced here: 68.1 us
  Pallas kernels  59.6 us (87%)
  local copies, waits for them, and re-layouts  3.97 us (6%)
  matrix products  2.19 us (3%)
  other arithmetic  1.72 us (3%)
    pallas_call x1, Pallas kernels, body(): pl.pallas_call(functools.partial(kernel, nc, nf), out_shape=(jax.ShapeDty...  59.6 us
    dot_general x1, matrix products, project_tiles(): lax.dot_general(table, values, (((0,), (1,)), ((), ())), preferred_elemen...  2.19 us
    unnamed x1, local copies, waits for them, and re-layouts  1.67 us
    pallas_call x1, local copies, waits for them, and re-layouts, body(): pl.pallas_call(functools.partial(kernel, nc, nf), out_shape=(jax.ShapeDty...  1.52 us

profile of v1, /device:TPU:0, one launch (start us, length us, event | category | flops | bytes accessed | tf_op | source)
XLA Modules:
  0.0 68.1 jit_solution(9987789204851808811)
XLA Ops:
  0.6 0.8 %reshape.41 = bf16[4,128,32]{1,0,2:T(4,128)(2,1)S(1)} reshape(bf16[512,32]{0,1:T(8,128)(2,1)} %param.16) | data formatting | bytes 65536 | tf_op jit(solution)/shard_map/reshape | solution.py:26
  1.4 0.7 %fusion.5 = f32[4,4096]{1,0:T(4,128)S(1)} fusion(s32[4096]{0:T(1024)} %param.13), kind=kLoop, calls=%fused_computation.7 | loop fusion | flops 32768 | bytes 81920 | tf_op jit(solution)/shard_map/convert_element_type | solution.py:30
  2.2 2.2 %fusion.1 = f32[4096,128]{0,1:T(8,128)S(1)} fusion(bf16[128,128]{0,1:T(8,128)(2,1)S(1)} %bitcast.14, bf16[4096,128]{1,0:T(8,128)(2,1)} %param.9, s32[4096]{0:T(1024)} %param.10), kind=kOutput, calls=%fused_computation.3 | convolution fusion | flops 135266304 | bytes 3194880 | tf_op jit(solution)/shard_map/dot_general | solution.py:27
  4.4 1.0 %multiply_reduce_fusion.proj_ref = f32[32,4096]{1,0:T(8,128)} fusion(f32[4,32,4096]{2,1,0:T(8,128)S(1)} %bitcast.13, f32[4,4096]{1,0:T(4,128)S(1)} %fusion.5), kind=kLoop, calls=%fused_computation | loop fusion | flops 917504 | bytes 2686976 | tf_op jit(solution)/shard_map/reduce_sum | solution.py:31
  5.3 59.6 %shard_map.104 = (bf16[128,1024]{1,0:T(8,128)(2,1)}, f32[128,32]{1,0:T(8,128)}) custom-call(f32[32,4096]{1,0:T(8,128)} %multiply_reduce_fusion.proj_ref, s32[1,4096]{1,0:T(1,128)} %bitcast.16, s32[1,4096]{1,0:T(1,128)} %bitcast.17, s32[1,4096]{1,0:T(1,128)} %bitcast.18, bf16[32,256]{1,0:T(8,128)(2,1)} %bitcast.19, bf16[32,128]{1,0:T(8,128)(2,1)} %bitcast.20), custom_call_target="tpu_custom_call" | custom-call | tf_op jit(solution)/shard_map/pallas_call | solution.py:382
  64.9 1.5 %copy.14 = f32[128,32]{0,1:T(8,128)} copy(f32[128,32]{1,0:T(8,128)} %get-tuple-element.7) | data formatting | bytes 32768 | tf_op jit(solution)/shard_map/pallas_call | solution.py:382
  66.4 1.7 %copy.16 = bf16[128,1024]{1,0:T(8,128)(2,1)} copy(bf16[128,1024]{1,0:T(8,128)(2,1)} %get-tuple-element.10) | data formatting | bytes 524288
  (1 shorter events, 0.0 us)

commit v2 on v1

--- a/solution.py
+++ b/solution.py
@@ -47,12 +47,12 @@
     slots,
     masked,
     send,
+    send_key,
     got,
-    kh,
-    kl,
+    got_key,
+    got_f1,
     acc,
     sib,
-    xrecv,
     gram,
     grecv,
     gown,
@@ -60,10 +60,10 @@
     gfull,
     a2a_send,
     a2a_recv,
+    x_send,
+    x_recv,
     sib_send,
     sib_recv,
-    x_send,
-    x_recv,
     g_send,
     g_recv,
     b_send,
@@ -71,8 +71,7 @@
 ):
     tiles = proj_ref.shape[1]
     r3 = proj_ref.shape[0]
-    r1 = f1_ref.shape[0]
-    r2 = f2_ref.shape[0]
+    r1, i1 = f1_ref.shape
     feats = data.shape[0]
     cap = tiles // nf
     br = f2_ref.shape[1]
@@ -99,9 +98,34 @@
             barrier, inc=1, device_id=(other // nf, lax.rem(other, nf)), device_id_type=MESH
         )
 
+    def a2a_copy(what, j):
+        source = (send.at[j], send_key.at[j], f1_ref)[what]
+        place_there = (got, got_key, got_f1)[what].at[0, j]
+        return pltpu.make_async_remote_copy(
+            src_ref=source,
+            dst_ref=place_there,
+            send_sem=a2a_send.at[what, j],
+            recv_sem=a2a_recv.at[what, j],
+            device_id=(q, lax.rem(f + j, nf)),
+            device_id_type=MESH,
+        )
+
+    def x_copy(what, dx, j):
+        where = (got, got_key, got_f1)[what]
+        return pltpu.make_async_remote_copy(
+            src_ref=where.at[0, j],
+            dst_ref=where.at[dx, j],
+            send_sem=x_send.at[what, dx, j],
+            recv_sem=x_recv.at[what, dx, j],
+            device_id=(lax.rem(x + dx, nx) * 2 + c, f),
+            device_id_type=MESH,
+        )
+
     groups = lax.broadcasted_iota(jnp.int32, (nf, tiles), 0)
     owner = row_ref[...] // br
     member[...] = jnp.where(groups == owner, 1.0, 0.0)
+    got_f1[0, 0] = f1_ref[...]
+    acc[...] = jnp.zeros_like(acc)
     stacked = jnp.concatenate(
         [member[:, k * CHUNK : (k + 1) * CHUNK] for k in range(chunks)], axis=0
     )
@@ -112,6 +136,12 @@
         jnp.where(early < late, 1.0, 0.0).astype(jnp.bfloat16),
         preferred_element_type=jnp.float32,
     )
+    pl.semaphore_wait(barrier, ndev - 1)
+
+    @pl.loop(1, nf)
+    def _(j):
+        a2a_copy(2, j).start()
+
     carry = jnp.zeros((nf, 1), jnp.float32)
     for k in range(chunks):
         cols = slice(k * CHUNK, (k + 1) * CHUNK)
@@ -123,97 +153,61 @@
         high = value.astype(jnp.bfloat16)
         data[0:r3, cols] = high
         data[r3 : 2 * r3, cols] = (value - high.astype(jnp.float32)).astype(jnp.bfloat16)
-        data[2 * r3 : 2 * r3 + r1, cols] = jnp.dot(
-            f1_ref[...],
-            onehot(f1_ref.shape[1], first_ref[:, cols]),
-            preferred_element_type=jnp.float32,
-        ).astype(jnp.bfloat16)
         kind = lax.broadcasted_iota(jnp.int32, (16, CHUNK), 0)
-        rows = row_ref[:, cols]
-        marks = jnp.where(kind == 0, dest_ref[:, cols], jnp.where(kind == 1, rows % br, 0))
-        data[2 * r3 + r1 :, cols] = marks.astype(jnp.float32).astype(jnp.bfloat16)
-
-    def a2a_copy(j):
-        to = lax.rem(f + j, nf)
-        return pltpu.make_async_remote_copy(
-            src_ref=send.at[j],
-            dst_ref=got.at[j],
-            send_sem=a2a_send.at[j],
-            recv_sem=a2a_recv.at[j],
-            device_id=(q, to),
-            device_id_type=MESH,
-        )
-
-    def place(first_step):
+        marks = jnp.where(
+            kind == 0,
+            dest_ref[:, cols],
+            jnp.where(
+                kind == 1,
+                row_ref[:, cols] % br,
+                jnp.where(kind == 2, first_ref[:, cols], 0),
+            ),
+        )
+        data[2 * r3 :, cols] = marks.astype(jnp.float32).astype(jnp.bfloat16)
+
+    @pl.loop(0, nf // 2)
+    def _(pair):
         for half in range(2):
-            group = lax.rem(f + first_step + half, nf)
+            group = lax.rem(f + nf // 2 + 2 * pair + half, nf)
             masked[half * feats : (half + 1) * feats, :] = data[...] * member[
                 pl.ds(group, 1), :
             ].astype(jnp.bfloat16)
-        return lax.dot_general(
+        placed = lax.dot_general(
             masked[...], slots[...], NT, preferred_element_type=jnp.float32
-        ).astype(jnp.bfloat16)
-
-    pl.semaphore_wait(barrier, ndev - 1)
-
-    @pl.loop(0, nf // 2)
-    def _(pair):
-        j = 2 * pair + 1
-        placed = place(j)
-        send[j] = placed[:feats]
-        a2a_copy(j).start()
-
-        @pl.when(pair < nf // 2 - 1)
-        def _():
-            send[j + 1] = placed[feats:]
-            a2a_copy(j + 1).start()
-
-        @pl.when(pair == nf // 2 - 1)
-        def _():
-            got[0] = placed[feats:]
-
-    def target(j, xs):
-        marks = got[j, 2 * r3 + r1 :, :].astype(jnp.float32)
-        key = (marks[0:1] - (2 * xs).astype(jnp.float32)) * br + marks[1:2]
-        return onehot(2 * br, key)
-
-    def add(slot, rows, total, fresh):
+        )
         for half in range(2):
-            new = total[:, half * br : (half + 1) * br]
-            if fresh:
-                acc[slot, half, rows, :] = new
+            j = lax.rem(nf // 2 + 2 * pair + half, nf)
+            block = placed[half * feats : (half + 1) * feats]
+            values = block[: 2 * r3].astype(jnp.bfloat16)
+            marks = block[2 * r3 : 2 * r3 + 3]
+            key = (marks[0:1] * br + marks[1:2]) * i1 + marks[2:3]
+
+            def leave():
+                send[j] = values
+                send_key[j] = key
+                a2a_copy(0, j).start()
+                a2a_copy(1, j).start()
+
+            def stay():
+                got[0, 0] = values
+                got_key[0, 0] = key
+
+            if half:
+                leave()
             else:
-                acc[slot, half, rows, :] += new
-
-    def sib_copy(slot, k):
-        rows = pl.ds(k * part, part)
-        return pltpu.make_async_remote_copy(
-            src_ref=acc.at[slot, 1 - c, rows],
-            dst_ref=sib.at[slot, rows],
-            send_sem=sib_send.at[slot, k],
-            recv_sem=sib_recv.at[slot, k],
-            device_id=(x * 2 + 1 - c, f),
-            device_id_type=MESH,
-        )
-
-    def x_copy(slot, k):
-        rows = pl.ds(k * part, part)
-        return pltpu.make_async_remote_copy(
-            src_ref=acc.at[slot, c, rows],
-            dst_ref=xrecv.at[slot, rows],
-            send_sem=x_send.at[slot, k],
-            recv_sem=x_recv.at[slot, k],
-            device_id=(lax.rem(x + slot, nx) * 2 + c, f),
-            device_id_type=MESH,
-        )
+                pl.when(j != 0)(leave)
+                pl.when(j == 0)(stay)
 
     per = part // r3
-    first_slot = 1 % nx
-
-    def arrive(j, fresh):
-        sel = target(j, lax.rem(x + first_slot, nx))
-        value = got[j, 0:r3, :].astype(jnp.float32) + got[j, r3 : 2 * r3, :].astype(jnp.float32)
-        fr = got[j, 2 * r3 : 2 * r3 + r1, :].astype(jnp.float32)
+
+    def arrive(dx, j):
+        key = got_key[dx, j]
+        target = jnp.floor(key * (1.0 / i1))
+        fr = jnp.dot(
+            got_f1[dx, j], onehot(i1, key - target * i1), preferred_element_type=jnp.float32
+        )
+        sel = onehot(2 * br, target - (2 * x * br).astype(jnp.float32))
+        value = got[dx, j, 0:r3, :].astype(jnp.float32) + got[dx, j, r3:, :].astype(jnp.float32)
         for k in range(PARTS):
             rows = pl.ds(k * part, part)
             prod = jnp.concatenate(
@@ -221,57 +215,57 @@
             )
             high = prod.astype(jnp.bfloat16)
             low = (prod - high.astype(jnp.float32)).astype(jnp.bfloat16)
-            kh[j, rows, :] = high
-            kl[j, rows, :] = low
             total = lax.dot_general(
                 high, sel, NT, preferred_element_type=jnp.float32
             ) + lax.dot_general(low, sel, NT, preferred_element_type=jnp.float32)
-            add(first_slot, rows, total, fresh)
-
-    arrive(0, True)
-
-    @pl.loop(1, nf)
-    def _(j):
-        a2a_copy(j).wait()
-        arrive(j, False)
-
-    def exchange(slot):
-        for k in range(PARTS):
-            sib_copy(slot, k).start()
-
-    def forward(slot):
-        for k in range(PARTS):
-            rows = pl.ds(k * part, part)
-            sib_copy(slot, k).wait()
-            acc[slot, c, rows, :] += sib[slot, rows, :]
-            if slot:
-                x_copy(slot, k).start()
-
-    def again(slot):
-        @pl.loop(0, PARTS)
-        def _(k):
-            rows = pl.ds(pl.multiple_of(k * part, part), part)
-            for j in range(nf):
-                sel = target(j, lax.rem(x + slot, nx))
-                total = lax.dot_general(
-                    kh[j, rows, :], sel, NT, preferred_element_type=jnp.float32
-                ) + lax.dot_general(kl[j, rows, :], sel, NT, preferred_element_type=jnp.float32)
-                add(slot, rows, total, j == 0)
-
-    exchange(first_slot)
-    forward(first_slot)
-    for slot in list(range(2, nx)) + ([0] if nx > 1 else []):
-        again(slot)
-        exchange(slot)
-        forward(slot)
-
+            for half in range(2):
+                acc[half, rows, :] += total[:, half * br : (half + 1) * br]
+
+    def turn(i):
+        j = lax.rem(i + nf // 2 - 1 + i // (nf // 2 + 1), nf)
+        return j * (1 - (nf - i) // nf)
+
+    @pl.loop(0, nf + 1)
+    def _(i):
+        @pl.when(i < nf)
+        def _():
+            j = turn(i)
+
+            @pl.when(i > 0)
+            def _():
+                for what in (2, 0, 1):
+                    a2a_copy(what, j).wait()
+
+            for dx in range(1, nx):
+                for what in (2, 0, 1):
+                    x_copy(what, dx, j).start()
+            arrive(0, j)
+
+        @pl.when(i > 0)
+        def _():
+            j = turn(i - 1)
+            for dx in range(1, nx):
+                for what in (2, 0, 1):
+                    x_copy(what, dx, j).wait()
+                arrive(dx, j)
+
+    def sib_copy(k):
+        rows = pl.ds(k * part, part)
+        return pltpu.make_async_remote_copy(
+            src_ref=acc.at[1 - c, rows],
+            dst_ref=sib.at[rows],
+            send_sem=sib_send.at[k],
+            recv_sem=sib_recv.at[k],
+            device_id=(x * 2 + 1 - c, f),
+            device_id_type=MESH,
+        )
+
+    for k in range(PARTS):
+        sib_copy(k).start()
     for k in range(PARTS):
         rows = pl.ds(k * part, part)
-        for slot in range(1, nx):
-            x_copy(slot, k).wait()
-        total = acc[0, c, rows, :]
-        for slot in range(1, nx):
-            total = total + xrecv[slot, rows, :]
+        sib_copy(k).wait()
+        total = acc[c, rows, :] + sib[rows, :]
         ttmc_ref[:, k * part : (k + 1) * part] = total.T.astype(jnp.bfloat16)
 
     ttmc = ttmc_ref[...]
@@ -369,7 +363,8 @@
     cap = tiles // nf
     width = r1 * r3
     nx = nc // 2
-    feats = 2 * r3 + r1 + 16
+    i1 = factor_one.shape[0]
+    feats = 2 * r3 + 16
     pieces = (r2 // 8) * (width // 128)
     positions = jnp.arange(FIBER, dtype=jnp.int32)
     masked = jnp.where(
@@ -392,24 +387,24 @@
             pltpu.VMEM((nf, tiles), f32),
             pltpu.VMEM((cap, tiles), bf16),
             pltpu.VMEM((2 * feats, tiles), bf16),
-            pltpu.VMEM((nf, feats, cap), bf16),
-            pltpu.VMEM((nf, feats, cap), bf16),
-            pltpu.VMEM((nf, width, cap), bf16),
-            pltpu.VMEM((nf, width, cap), bf16),
-            pltpu.VMEM((nx, 2, width, br), f32),
-            pltpu.VMEM((nx, width, br), f32),
-            pltpu.VMEM((nx, width, br), f32),
+            pltpu.VMEM((nf, 2 * r3, cap), bf16),
+            pltpu.VMEM((nf, 1, cap), f32),
+            pltpu.VMEM((nx, nf, 2 * r3, cap), bf16),
+            pltpu.VMEM((nx, nf, 1, cap), f32),
+            pltpu.VMEM((nx, nf, r1, i1), bf16),
+            pltpu.VMEM((2, width, br), f32),
+            pltpu.VMEM((width, br), f32),
             pltpu.VMEM((pieces, 8, 128), f32),
             pltpu.VMEM((nc * nf, 8, 128), f32),
             pltpu.VMEM((8, 128), f32),
             pltpu.VMEM((pieces, 8, 128), f32),
             pltpu.VMEM((r2, width), f32),
-            dma((nf,)),
-            dma((nf,)),
-            dma((nx, PARTS)),
-            dma((nx, PARTS)),
-            dma((nx, PARTS)),
-            dma((nx, PARTS)),
+            dma((3, nf)),
+            dma((3, nf)),
+            dma((3, nx, nf)),
+            dma((3, nx, nf)),
+            dma((PARTS,)),
+            dma((PARTS,)),
             dma,
             dma,
             dma,

time: 68.5 us -> 62.2 us (0.908)
  Pallas kernels: 59.6 us -> 53.3 us
    pallas_call x1, Pallas kernels: 59.6 us -> 53.3 us  [body(): pl.pallas_call(functools.partial(kernel, nc, nf), out_shape=(jax.ShapeDty...]
where the time goes in v2:
time: 62.2 us; the launch traced here: 61.9 us
  Pallas kernels  53.3 us (86%)
  local copies, waits for them, and re-layouts  3.97 us (6%)
  matrix products  2.19 us (4%)
  other arithmetic  1.72 us (3%)
  between operations  0.66 us (1%)
    pallas_call x1, Pallas kernels, body(): pl.pallas_call(functools.partial(kernel, nc, nf), out_shape=(jax.ShapeDty...  53.3 us
    dot_general x1, matrix products, project_tiles(): lax.dot_general(table, values, (((0,), (1,)), ((), ())), preferred_elemen...  2.19 us
    unnamed x1, local copies, waits for them, and re-layouts  1.67 us
    pallas_call x1, local copies, waits for them, and re-layouts, body(): pl.pallas_call(functools.partial(kernel, nc, nf), out_shape=(jax.ShapeDty...  1.52 us

profile of v2, /device:TPU:0, one launch (start us, length us, event | category | flops | bytes accessed | tf_op | source)
XLA Modules:
  0.0 61.9 jit_solution(6178567599848311438)
XLA Ops:
  0.6 0.8 %reshape.41 = bf16[4,128,32]{1,0,2:T(4,128)(2,1)S(1)} reshape(bf16[512,32]{0,1:T(8,128)(2,1)} %param.16) | data formatting | bytes 65536 | tf_op jit(solution)/shard_map/reshape | solution.py:26
  1.4 0.7 %fusion.5 = f32[4,4096]{1,0:T(4,128)S(1)} fusion(s32[4096]{0:T(1024)} %param.13), kind=kLoop, calls=%fused_computation.7 | loop fusion | flops 32768 | bytes 81920 | tf_op jit(solution)/shard_map/convert_element_type | solution.py:30
  2.2 2.2 %fusion.1 = f32[4096,128]{0,1:T(8,128)S(1)} fusion(bf16[128,128]{0,1:T(8,128)(2,1)S(1)} %bitcast.14, bf16[4096,128]{1,0:T(8,128)(2,1)} %param.9, s32[4096]{0:T(1024)} %param.10), kind=kOutput, calls=%fused_computation.3 | convolution fusion | flops 135266304 | bytes 3194880 | tf_op jit(solution)/shard_map/dot_general | solution.py:27
  4.4 1.0 %multiply_reduce_fusion.proj_ref = f32[32,4096]{1,0:T(8,128)} fusion(f32[4,32,4096]{2,1,0:T(8,128)S(1)} %bitcast.13, f32[4,4096]{1,0:T(4,128)S(1)} %fusion.5), kind=kLoop, calls=%fused_computation | loop fusion | flops 917504 | bytes 2686976 | tf_op jit(solution)/shard_map/reduce_sum | solution.py:31
  5.3 53.3 %shard_map.104 = (bf16[128,1024]{1,0:T(8,128)(2,1)}, f32[128,32]{1,0:T(8,128)}) custom-call(f32[32,4096]{1,0:T(8,128)} %multiply_reduce_fusion.proj_ref, s32[1,4096]{1,0:T(1,128)} %bitcast.16, s32[1,4096]{1,0:T(1,128)} %bitcast.17, s32[1,4096]{1,0:T(1,128)} %bitcast.18, bf16[32,256]{1,0:T(8,128)(2,1)} %bitcast.19, bf16[32,128]{1,0:T(8,128)(2,1)} %bitcast.20), custom_call_target="tpu_custom_call" | custom-call | tf_op jit(solution)/shard_map/pallas_call | solution.py:377
  58.7 1.5 %copy.14 = f32[128,32]{0,1:T(8,128)} copy(f32[128,32]{1,0:T(8,128)} %get-tuple-element.7) | data formatting | bytes 32768 | tf_op jit(solution)/shard_map/pallas_call | solution.py:377
  60.2 1.7 %copy.16 = bf16[128,1024]{1,0:T(8,128)(2,1)} copy(bf16[128,1024]{1,0:T(8,128)(2,1)} %get-tuple-element.10) | data formatting | bytes 524288
  (1 shorter events, 0.0 us)

commit v3 on v2

--- a/solution.py
+++ b/solution.py
@@ -165,10 +165,14 @@
         )
         data[2 * r3 :, cols] = marks.astype(jnp.float32).astype(jnp.bfloat16)
 
+    def step_of(pair):
+        late = (pair + nf // 2 - 1) // (nf // 2)
+        return late * (2 + lax.rem(2 * (pair - 1) + nf // 2 - 2 + nf - 2, nf - 2))
+
     @pl.loop(0, nf // 2)
     def _(pair):
         for half in range(2):
-            group = lax.rem(f + nf // 2 + 2 * pair + half, nf)
+            group = lax.rem(f + step_of(pair) + half, nf)
             masked[half * feats : (half + 1) * feats, :] = data[...] * member[
                 pl.ds(group, 1), :
             ].astype(jnp.bfloat16)
@@ -176,7 +180,7 @@
             masked[...], slots[...], NT, preferred_element_type=jnp.float32
         )
         for half in range(2):
-            j = lax.rem(nf // 2 + 2 * pair + half, nf)
+            j = step_of(pair) + half
             block = placed[half * feats : (half + 1) * feats]
             values = block[: 2 * r3].astype(jnp.bfloat16)
             marks = block[2 * r3 : 2 * r3 + 3]
@@ -191,12 +195,24 @@
             def stay():
                 got[0, 0] = values
                 got_key[0, 0] = key
+                for dx in range(1, nx):
+                    for what in range(2):
+                        x_copy(what, dx, 0).start()
 
             if half:
                 leave()
             else:
                 pl.when(j != 0)(leave)
                 pl.when(j == 0)(stay)
+
+    for dx in range(1, nx):
+        x_copy(2, dx, 0).start()
+
+    @pl.loop(1, nf)
+    def _(j):
+        a2a_copy(2, j).wait()
+        for dx in range(1, nx):
+            x_copy(2, dx, j).start()
 
     per = part // r3
 
@@ -222,8 +238,7 @@
                 acc[half, rows, :] += total[:, half * br : (half + 1) * br]
 
     def turn(i):
-        j = lax.rem(i + nf // 2 - 1 + i // (nf // 2 + 1), nf)
-        return j * (1 - (nf - i) // nf)
+        return step_of(i // 2) + lax.rem(i, 2)
 
     @pl.loop(0, nf + 1)
     def _(i):
@@ -233,12 +248,12 @@
 
             @pl.when(i > 0)
             def _():
-                for what in (2, 0, 1):
+                for what in range(2):
                     a2a_copy(what, j).wait()
-
-            for dx in range(1, nx):
-                for what in (2, 0, 1):
-                    x_copy(what, dx, j).start()
+                for dx in range(1, nx):
+                    for what in range(2):
+                        x_copy(what, dx, j).start()
+
             arrive(0, j)
 
         @pl.when(i > 0)
@@ -331,7 +346,7 @@
         a, b = p // lanes, p % lanes
         gfull[a * 8 : (a + 1) * 8, b * 128 : (b + 1) * 128] = gall[p]
     out_ref[...] = lax.dot_general(
-        ttmc, gfull[...].astype(jnp.bfloat16), NT, preferred_element_type=jnp.float32
+        gfull[...].astype(jnp.bfloat16), ttmc, NT, preferred_element_type=jnp.float32
     ) / 32.0
 
     @pl.when(owns)
@@ -374,11 +389,11 @@
     vmem = pl.BlockSpec(memory_space=pltpu.VMEM)
     bf16, f32 = jnp.bfloat16, jnp.float32
     dma = pltpu.SemaphoreType.DMA
-    return pl.pallas_call(
+    ttmc, projected = pl.pallas_call(
         functools.partial(kernel, nc, nf),
         out_shape=(
             jax.ShapeDtypeStruct((br, width), bf16),
-            jax.ShapeDtypeStruct((br, r2), f32),
+            jax.ShapeDtypeStruct((r2, br), f32),
         ),
         in_specs=[vmem] * 6,
         out_specs=(vmem, vmem),
@@ -421,6 +436,7 @@
         factor_one.T,
         factor_two.T,
     )
+    return ttmc, projected.T
 
 
 def solution(mesh):

time: 62.2 us -> 60.4 us (0.971)
  Pallas kernels: 53.3 us -> 51.7 us
    pallas_call x1, Pallas kernels: 53.3 us -> 51.7 us  [body(): pl.pallas_call(functools.partial(kernel, nc, nf), out_shape=(jax.ShapeDty...]
    pallas_call x1 -> x0, local copies, waits for them, and re-layouts: 1.52 us -> none  [body(): pl.pallas_call(functools.partial(kernel, nc, nf), out_shape=(jax.ShapeDty...]
    unnamed x1 -> x2, local copies, waits for them, and re-layouts: 1.67 us -> 2.99 us
where the time goes in v3:
time: 60.4 us; the launch traced here: 60 us
  Pallas kernels  51.7 us (86%)
  local copies, waits for them, and re-layouts  3.77 us (6%)
  matrix products  2.19 us (4%)
  other arithmetic  1.72 us (3%)
  between operations  0.66 us (1%)
    pallas_call x1, Pallas kernels, body(): pl.pallas_call(functools.partial(kernel, nc, nf), out_shape=(jax.ShapeDty...  51.7 us
    unnamed x2, local copies, waits for them, and re-layouts  2.99 us
    dot_general x1, matrix products, project_tiles(): lax.dot_general(table, values, (((0,), (1,)), ((), ())), preferred_elemen...  2.19 us

profile of v3, /device:TPU:0, one launch (start us, length us, event | category | flops | bytes accessed | tf_op | source)
XLA Modules:
  0.0 60.0 jit_solution(5127652284162514287)
XLA Ops:
  0.6 0.8 %reshape.41 = bf16[4,128,32]{1,0,2:T(4,128)(2,1)S(1)} reshape(bf16[512,32]{0,1:T(8,128)(2,1)} %param.16) | data formatting | bytes 65536 | tf_op jit(solution)/shard_map/reshape | solution.py:26
  1.4 0.7 %fusion.5 = f32[4,4096]{1,0:T(4,128)S(1)} fusion(s32[4096]{0:T(1024)} %param.13), kind=kLoop, calls=%fused_computation.7 | loop fusion | flops 32768 | bytes 81920 | tf_op jit(solution)/shard_map/convert_element_type | solution.py:30
  2.2 2.2 %fusion.1 = f32[4096,128]{0,1:T(8,128)S(1)} fusion(bf16[128,128]{0,1:T(8,128)(2,1)S(1)} %bitcast.15, bf16[4096,128]{1,0:T(8,128)(2,1)} %param.9, s32[4096]{0:T(1024)} %param.10), kind=kOutput, calls=%fused_computation.3 | convolution fusion | flops 135266304 | bytes 3194880 | tf_op jit(solution)/shard_map/dot_general | solution.py:27
  4.4 1.0 %multiply_reduce_fusion.proj_ref = f32[32,4096]{1,0:T(8,128)} fusion(f32[4,32,4096]{2,1,0:T(8,128)S(1)} %bitcast.14, f32[4,4096]{1,0:T(4,128)S(1)} %fusion.5), kind=kLoop, calls=%fused_computation | loop fusion | flops 917504 | bytes 2686976 | tf_op jit(solution)/shard_map/reduce_sum | solution.py:31
  5.3 51.7 %shard_map.104 = (bf16[128,1024]{1,0:T(8,128)(2,1)}, f32[32,128]{1,0:T(8,128)}) custom-call(f32[32,4096]{1,0:T(8,128)} %multiply_reduce_fusion.proj_ref, s32[1,4096]{1,0:T(1,128)} %bitcast.17, s32[1,4096]{1,0:T(1,128)} %bitcast.18, s32[1,4096]{1,0:T(1,128)} %bitcast.19, bf16[32,256]{1,0:T(8,128)(2,1)} %bitcast.20, bf16[32,128]{1,0:T(8,128)(2,1)} %bitcast.22), custom_call_target="tpu_custom_call" | custom-call | tf_op jit(solution)/shard_map/pallas_call | solution.py:392
  57.0 1.7 %copy.14 = bf16[128,1024]{1,0:T(8,128)(2,1)} copy(bf16[128,1024]{1,0:T(8,128)(2,1)} %get-tuple-element.8) | data formatting | bytes 524288
  58.7 1.3 %copy.15 = f32[128,32]{0,1:T(8,128)} copy(f32[128,32]{0,1:T(8,128)} %bitcast.21) | data formatting | bytes 32768
  (1 shorter events, 0.0 us)
